TPU v7x, 32 devices: a whole 2x2x4 slice. The times are simulated.
32 devices in a mesh: tower: 2 (over core), dp: 16 (over z, y, x).
Axes of the slice: x: 2, y: 2, z: 4, core: 2. Of those that a mesh axis runs over, the one named last changes fastest.
Arguments:
- tokens: bfloat16 [2, 8192, 768], P('tower', 'dp'), may hold values from -6 to 6
- doc_ids: int32 [2, 8192], P('tower', 'dp'), may hold values from 0 to 11, as said below
- pad_mask: int32 [2, 8192], P('tower', 'dp'), may hold values 0 or 1
- targets: int32 [12], replicated, may hold values from 0 to 11, each once
- w_qkv: bfloat16 [768, 2304], replicated, may hold values from -0.21875 to 0.21875
- w_out: bfloat16 [768, 768], replicated, may hold values from -0.875 to 0.875
- ln1_gain: float32 [768], replicated, may hold values from 0.5 to 1.5
- ln1_bias: float32 [768], replicated, may hold values from -0.6 to 0.6
- w_gate: bfloat16 [768, 3072], replicated, may hold values from -0.21875 to 0.21875
- w_up: bfloat16 [768, 3072], replicated, may hold values from -0.21875 to 0.21875
- w_down: bfloat16 [3072, 768], replicated, may hold values from -0.109375 to 0.109375
- ln2_gain: float32 [768], replicated, may hold values from 0.5 to 1.5
- ln2_bias: float32 [768], replicated, may hold values from -0.6 to 0.6
Outputs:
- scores: float32 [12, 12], replicated
- loss: float32 [], replicated
- token_grad: float32 [2, 8192, 768], P('tower', 'dp')
- w_qkv_grad: float32 [768, 2304], P('dp')
- w_out_grad: float32 [768, 768], P('dp')
- ln1_gain_grad: float32 [768], P('dp')
- ln1_bias_grad: float32 [768], P('dp')
- w_gate_grad: float32 [768, 3072], P('dp')
- w_up_grad: float32 [768, 3072], P('dp')
- w_down_grad: float32 [3072, 768], P('dp')
- ln2_gain_grad: float32 [768], P('dp')
- ln2_bias_grad: float32 [768], P('dp')
Inputs may be any that keep to these rules, and one draw needn't show every extreme that they name: `doc_ids`: within each tower the ids never fall; the k-th aligned group of 2048 slots holds exactly the documents k * 3 to k * 3 + 2, one of them exactly 1024 slots long. `targets`: each document of the second tower is the target of exactly one query.
All inputs are finite; a program needn't handle non-finite values. No bound on the sum of `pad_mask` on one device may be relied on, other than what follows from the above.
Results may differ from a plain program's by a relative error of at most 0.015.
Values may be sent and summed in bfloat16 or wider, within the bound.
A program may use at most 192 MiB of HBM per device.

v0:
```python
import jax
import jax.numpy as jnp
from jax import lax
from jax.sharding import PartitionSpec as P

HEADS = 12
HEAD_DIM = 64
SPAN = 4
DOCS_GRP = 3
precise = lax.Precision.HIGHEST
norm_eps = 1e-05


def swapped(value, axis, bit):
    return lax.ppermute(value, axis, [(i, i ^ 1 << bit) for i in range(lax.axis_size(axis))])


def for_sending(value):
    return jax.tree.map(lambda a: a.astype(jnp.bfloat16) if a.dtype == jnp.float32 else a, value)


def angles_for(positions, half):
    freqs = 1000.0 ** (-jnp.arange(half, dtype=jnp.float32) / half)
    theta = positions.astype(jnp.float32)[:, None] * freqs[None, :]
    return (jnp.cos(theta)[:, None, :], jnp.sin(theta)[:, None, :])


def rotate(values, cosine, sine):
    half = values.shape[-1] // 2
    upper = values[..., :half]
    lower = values[..., half:]
    return jnp.concatenate([upper * cosine - lower * sine, lower * cosine + upper * sine], -1)


def unrotate(values, cosine, sine):
    half = values.shape[-1] // 2
    upper = values[..., :half]
    lower = values[..., half:]
    return jnp.concatenate([upper * cosine + lower * sine, lower * cosine - upper * sine], -1)


def norm_rows(values, gain, bias):
    centred = values - jnp.mean(values, -1, keepdims=True)
    spread = jnp.mean(centred * centred, -1, keepdims=True)
    scale = lax.rsqrt(spread + norm_eps)
    normed = centred * scale
    return (normed * gain + bias, normed, scale)


def norm_back(grad, normed, scale, gain):
    shaped = grad * gain
    inner = (
        shaped
        - jnp.mean(shaped, -1, keepdims=True)
        - normed * jnp.mean(shaped * normed, -1, keepdims=True)
    )
    return (inner * scale, jnp.sum(grad * normed, 0), jnp.sum(grad, 0))


def contract_last(left, right):
    return lax.dot_general(
        left, right, (((1,), (1,)), ((), ())), preferred_element_type=jnp.float32
    )


def contract_first(left, right):
    return lax.dot_general(
        left, right, (((0,), (0,)), ((), ())), preferred_element_type=jnp.float32
    )


def local(
    tokens,
    doc_ids,
    pad_mask,
    targets,
    w_qkv,
    w_out,
    ln1_gain,
    ln1_bias,
    w_gate,
    w_up,
    w_down,
    ln2_gain,
    ln2_bias,
):
    width = w_out.shape[0]
    rows = tokens[0]
    count = rows.shape[0]
    tower = lax.axis_index("tower")
    place = lax.axis_index("dp")
    member_of = doc_ids[0] % DOCS_GRP
    live_row = pad_mask[0] == 1
    positions = place % SPAN * count + jnp.arange(count, dtype=jnp.int32)
    cosine, sine = angles_for(positions, HEAD_DIM // 2)
    mixed = jnp.dot(rows, w_qkv, preferred_element_type=jnp.float32)
    query = rotate(mixed[:, :width].reshape(count, HEADS, HEAD_DIM), cosine, sine).astype(
        jnp.bfloat16
    )
    keys = rotate(mixed[:, width : 2 * width].reshape(count, HEADS, HEAD_DIM), cosine, sine).astype(
        jnp.bfloat16
    )
    values = mixed[:, 2 * width :].astype(jnp.bfloat16)
    key_tags = jnp.where(live_row, member_of, -1).astype(jnp.bfloat16)
    group_keys = keys.reshape(count, width)
    group_values = values
    group_tags = key_tags
    levels = SPAN.bit_length() - 1
    for level in range(levels):
        other = swapped((group_keys, group_values, group_tags), "dp", level)
        group_keys = jnp.concatenate([group_keys, other[0]], 0)
        group_values = jnp.concatenate([group_values, other[1]], 0)
        group_tags = jnp.concatenate([group_tags, other[2]], 0)
    group_len = group_keys.shape[0]
    key_tag = group_tags.astype(jnp.float32)
    keys_heads = group_keys.reshape(group_len, HEADS, HEAD_DIM).transpose(1, 0, 2)
    values_heads = group_values.reshape(group_len, HEADS, HEAD_DIM).transpose(1, 0, 2)
    block = min(512, count)
    nblocks = count // block
    query_heads = query.transpose(1, 0, 2).reshape(HEADS, nblocks, block, HEAD_DIM)
    query_tag = member_of.astype(jnp.float32).reshape(nblocks, block)

    def head_scores(query_block, tag_block, head_keys):
        scores = contract_last(query_block, head_keys) * 0.125
        return jnp.where(tag_block[:, None] == key_tag[None, :], scores, -1e30)

    def attend_head(parts):
        head_query, head_keys, head_values = parts

        def attend_block(inputs):
            query_block, tag_block = inputs
            masked = head_scores(query_block, tag_block, head_keys)
            top = jnp.max(masked, -1, keepdims=True)
            expo = jnp.exp(masked - top)
            total = jnp.sum(expo, -1, keepdims=True)
            probs = (expo / total).astype(jnp.bfloat16)
            result = jnp.dot(probs, head_values, preferred_element_type=jnp.float32)
            return (result, (top + jnp.log(total))[:, 0])

        return lax.map(attend_block, (head_query, query_tag))

    outputs, log_totals = lax.map(attend_head, (query_heads, keys_heads, values_heads))
    attended = outputs.transpose(1, 2, 0, 3).reshape(count, width).astype(jnp.bfloat16)
    branch = jnp.dot(attended, w_out, preferred_element_type=jnp.float32)
    first, normed_one, scale_one = norm_rows(rows.astype(jnp.float32) + branch, ln1_gain, ln1_bias)
    inner = first.astype(jnp.bfloat16)
    gate = jnp.dot(inner, w_gate, preferred_element_type=jnp.float32)
    upper = jnp.dot(inner, w_up, preferred_element_type=jnp.float32)
    sigmoid = jax.nn.sigmoid(gate)
    activated = jax.nn.silu(gate)
    hidden = (activated * upper).astype(jnp.bfloat16)
    second, normed_two, scale_two = norm_rows(
        first + jnp.dot(hidden, w_down, preferred_element_type=jnp.float32), ln2_gain, ln2_bias
    )
    member = ((member_of[:, None] == jnp.arange(DOCS_GRP)[None, :]) & live_row[:, None]).astype(
        jnp.float32
    )
    sums = jnp.dot(member.T, second, precision=precise)
    group = place // SPAN
    part_sums = lax.all_gather(sums, "dp", axis=0, tiled=True)
    own_pooled = jnp.sum(part_sums.reshape(-1, SPAN, DOCS_GRP, width), 1).reshape(-1, width)
    own_embed = own_pooled * lax.rsqrt(jnp.sum(own_pooled * own_pooled, -1, keepdims=True) + 1e-06)
    embed = lax.all_gather(
        own_embed[None].astype(jnp.bfloat16), "tower", axis=0, tiled=True
    ).astype(jnp.float32)
    scores = jnp.dot(embed[0], embed[1].T, precision=precise) * 50.0
    docs = scores.shape[0]
    top = jnp.max(scores, -1, keepdims=True)
    log_sums = top[:, 0] + jnp.log(jnp.sum(jnp.exp(scores - top), -1))
    onehot = (jnp.arange(docs)[None, :] == targets[:, None]).astype(jnp.float32)
    chosen = jnp.sum(onehot * scores, -1)
    loss = jnp.mean(log_sums - chosen)
    grad_scores = (jnp.exp(scores - log_sums[:, None]) - onehot) / docs
    grad_query_embed = jnp.dot(grad_scores, embed[1], precision=precise) * 50.0
    grad_doc_embed = jnp.dot(grad_scores.T, embed[0], precision=precise) * 50.0
    own_grad = jnp.where(tower == 0, grad_query_embed, grad_doc_embed)
    start = group * DOCS_GRP
    grad_mine = lax.dynamic_slice_in_dim(own_grad, start, DOCS_GRP, 0)
    pooled_mine = lax.dynamic_slice_in_dim(own_pooled, start, DOCS_GRP, 0)
    inverse = lax.rsqrt(jnp.sum(pooled_mine * pooled_mine, -1, keepdims=True) + 1e-06)
    grad_pool = inverse * grad_mine - inverse**3 * pooled_mine * jnp.sum(
        pooled_mine * grad_mine, -1, keepdims=True
    )
    grad_second = jnp.dot(member, grad_pool, precision=precise)
    grad_h2, gain_two_grad, bias_two_grad = norm_back(grad_second, normed_two, scale_two, ln2_gain)
    grad_mlp = grad_h2.astype(jnp.bfloat16)
    w_down_grad = contract_first(hidden, grad_mlp)
    grad_hidden = contract_last(grad_mlp, w_down)
    grad_gate = (grad_hidden * upper * sigmoid * (1.0 + gate * (1.0 - sigmoid))).astype(
        jnp.bfloat16
    )
    grad_up = (grad_hidden * activated).astype(jnp.bfloat16)
    w_gate_grad = contract_first(inner, grad_gate)
    w_up_grad = contract_first(inner, grad_up)
    grad_first = grad_h2 + contract_last(grad_gate, w_gate) + contract_last(grad_up, w_up)
    grad_h1, gain_one_grad, bias_one_grad = norm_back(grad_first, normed_one, scale_one, ln1_gain)
    grad_branch = grad_h1.astype(jnp.bfloat16)
    w_out_grad = contract_first(attended, grad_branch)
    grad_attended = contract_last(grad_branch, w_out).astype(jnp.bfloat16)
    grad_heads = (
        grad_attended.reshape(count, HEADS, HEAD_DIM)
        .transpose(1, 0, 2)
        .reshape(HEADS, nblocks, block, HEAD_DIM)
    )

    def back_head(parts):
        head_query, head_keys, head_values, head_grad, head_totals = parts

        def back_block(carry, inputs):
            key_acc, value_acc = carry
            query_block, tag_block, grad_block, total_block = inputs
            masked = head_scores(query_block, tag_block, head_keys)
            probs = jnp.exp(masked - total_block[:, None])
            grad_probs = contract_last(grad_block, head_values)
            inner_sum = jnp.sum(probs * grad_probs, -1, keepdims=True)
            grad_logits = (probs * (grad_probs - inner_sum)).astype(jnp.bfloat16)
            grad_query_block = (
                jnp.dot(grad_logits, head_keys, preferred_element_type=jnp.float32) * 0.125
            )
            key_acc = key_acc + contract_first(grad_logits, query_block) * 0.125
            value_acc = value_acc + contract_first(probs.astype(jnp.bfloat16), grad_block)
            return ((key_acc, value_acc), grad_query_block)

        empty = jnp.zeros((group_len, HEAD_DIM), jnp.float32)
        (key_grad, value_grad), query_grad = lax.scan(
            back_block, (empty, empty), (head_query, query_tag, head_grad, head_totals)
        )
        return (key_grad, value_grad, query_grad)

    key_grads, value_grads, query_grads = lax.map(
        back_head, (query_heads, keys_heads, values_heads, grad_heads, log_totals)
    )
    key_full = key_grads.transpose(1, 0, 2).reshape(group_len, width)
    value_full = value_grads.transpose(1, 0, 2).reshape(group_len, width)
    for level in reversed(range(levels)):
        half = key_full.shape[0] // 2
        returned = swapped(
            (for_sending(key_full[half:]), for_sending(value_full[half:])), "dp", level
        )
        key_full = key_full[:half] + returned[0]
        value_full = value_full[:half] + returned[1]
    grad_query_rows = unrotate(
        query_grads.transpose(1, 2, 0, 3).reshape(count, HEADS, HEAD_DIM), cosine, sine
    )
    grad_key_rows = unrotate(key_full.reshape(count, HEADS, HEAD_DIM), cosine, sine)
    grad_mixed = jnp.concatenate(
        [grad_query_rows.reshape(count, width), grad_key_rows.reshape(count, width), value_full], 1
    ).astype(jnp.bfloat16)
    w_qkv_grad = contract_first(rows, grad_mixed)
    token_grad = grad_h1 + contract_last(grad_mixed, w_qkv)
    gain_grads = jnp.stack([gain_one_grad, bias_one_grad, gain_two_grad, bias_two_grad], 1)
    terms = (w_qkv_grad, w_out_grad, w_gate_grad, w_up_grad, w_down_grad, gain_grads)
    pieces = (
        lax.psum_scatter(terms[0], "dp", scatter_dimension=0, tiled=True),
        lax.psum_scatter(terms[1], "dp", scatter_dimension=0, tiled=True),
        lax.psum_scatter(terms[2], "dp", scatter_dimension=0, tiled=True),
        lax.psum_scatter(terms[3], "dp", scatter_dimension=0, tiled=True),
        lax.psum_scatter(terms[4], "dp", scatter_dimension=0, tiled=True),
        lax.psum_scatter(terms[5], "dp", scatter_dimension=0, tiled=True),
    )
    totals = (
        lax.psum(pieces[0].astype(jnp.bfloat16), "tower").astype(jnp.float32),
        lax.psum(pieces[1].astype(jnp.bfloat16), "tower").astype(jnp.float32),
        lax.psum(pieces[2].astype(jnp.bfloat16), "tower").astype(jnp.float32),
        lax.psum(pieces[3].astype(jnp.bfloat16), "tower").astype(jnp.float32),
        lax.psum(pieces[4].astype(jnp.bfloat16), "tower").astype(jnp.float32),
        lax.psum(pieces[5].astype(jnp.bfloat16), "tower").astype(jnp.float32),
    )
    gains_out = totals[5]
    return (
        scores,
        loss,
        token_grad[None],
        totals[0],
        totals[1],
        gains_out[:, 0],
        gains_out[:, 1],
        totals[2],
        totals[3],
        totals[4],
        gains_out[:, 2],
        gains_out[:, 3],
    )


def solution(mesh):
    placed = (
        P("tower", "dp", None),
        P("tower", "dp"),
        P("tower", "dp"),
        P(),
        P(),
        P(),
        P(),
        P(),
        P(),
        P(),
        P(),
        P(),
        P(),
    )
    return jax.shard_map(
        local,
        mesh=mesh,
        in_specs=placed,
        out_specs=(
            P(),
            P(),
            P("tower", "dp", None),
            P("dp", None),
            P("dp", None),
            P("dp"),
            P("dp"),
            P("dp", None),
            P("dp", None),
            P("dp", None),
            P("dp"),
            P("dp"),
        ),
        check_vma=False,
    )
```

profile of v0, /device:TPU:0, one launch (start us, length us, event | category | flops | bytes accessed | tf_op | source)
XLA Modules:
  0.0 1405.6 jit_solution(15379904082017169689)
XLA Ops:
  27.5 9.6 collective-permute-done.4
  41.8 11.2 collective-permute-done.2
  68.5 40.1 %collective-permute-done.1 = bf16[1024]{0:T(1024)(128)(2,1)} collective-permute-done((bf16[1024]{0:T(1024)(128)(2,1)S(1)}, bf16[1024]{0:T(1024)(128)(2,1)}, u32[]{:S(2)}, u32[]{:S(2)}) %collective-permute-start.1) | collective-permute-done | bytes 2080 | tf_op jit(solution)/shard_map/ppermute | solution.py:15
  117.6 6.6 copy.55
  128.1 6.6 copy.54
  134.7 71.9 %while.28 = (s32[]{:T(128)}, bf16[12,1,512,64]{2,3,1,0:T(8,128)(2,1)}, f32[12,1,512]{2,1,0:T(1,128)}, f32[1,512]{1,0:T(1,128)S(1)}, f32[2048]{0:T(1024)S(1)}, /*...) while((s32[]{:T(128)}, ...), condition=%wide.region_3.4_spmd.clone, body=%wide.region_0.3_spmd.sunk.clone | while | flops 277872128 | bytes 13926497 | solution.py:142
  210.1 5.1 fusion.98
  225.2 42.0 %all-gather = f32[16,3,768]{2,1,0:T(4,128)S(1)} all-gather(f32[1,3,768]{2,1,0:T(4,128)S(1)} %fusion.44), channel_id=1, replica_groups=mesh['tower'=2,'dp'=16] {'dp'}, dimensions={0}, use_global_device_ids=true | all-gather | bytes 156672 | tf_op jit(solution)/shard_map/all_gather | solution.py:160
  283.2 9.4 multiply_convert_fusion.1
  306.9 149.5 %while.29 = (s32[]{:T(128)}, f32[12,2048,64]{1,2,0:T(8,128)}, f32[12,2048,64]{1,2,0:T(8,128)}, f32[12,1,512,64]{2,3,1,0:T(8,128)}, f32[1,512]{1,0:T(1,128)}, /*i...) while((s32[]{:T(128)}, f32[12,2048,64]{1,2,0:T(8,128)}, ...), condition=%wide.region_22.23_spmd.clone, body=%wide.region_20.22_spmd.sunk.clone | while | flops 681737728 | bytes 34636948 | solution.py:230
  463.4 32.6 %collective-permute-done.6 = bf16[1024,768]{0,1:T(8,128)(2,1)S(1)} collective-permute-done((bf16[1024,768]{0,1:T(8,128)(2,1)S(1)}, bf16[1024,768]{0,1:T(8,128)(2,1)S(1)}, u32[]{:S(2)}, u32[]{:S(2)}) %collective-permute-start.6) | collective-permute-done | bytes 1572896 | tf_op jit(solution)/shard_map/ppermute | solution.py:15
  497.4 31.5 %collective-permute-done.8 = bf16[1024,768]{0,1:T(8,128)(2,1)S(1)} collective-permute-done((bf16[1024,768]{0,1:T(8,128)(2,1)S(1)}, bf16[1024,768]{0,1:T(8,128)(2,1)S(1)}, u32[]{:S(2)}, u32[]{:S(2)}) %collective-permute-start.8) | collective-permute-done | bytes 1572896 | tf_op jit(solution)/shard_map/ppermute | solution.py:15
  531.9 16.9 %collective-permute-done.9 = bf16[512,768]{0,1:T(8,128)(2,1)S(1)} collective-permute-done((bf16[512,768]{0,1:T(8,128)(2,1)S(1)}, bf16[512,768]{0,1:T(8,128)(2,1)S(1)}, u32[]{:S(2)}, u32[]{:S(2)}) %collective-permute-start.9) | collective-permute-done | bytes 786464 | tf_op jit(solution)/shard_map/ppermute | solution.py:15
  554.8 8.0 copy.64
  563.2 8.7 fusion.57
  571.9 8.4 fusion.101
  580.4 8.6 fusion.100
  595.0 115.7 %reduce-scatter.19.cloned.1.call-done = f32[48,2304]{1,0:T(8,128)} async-done(((f32[768,2304]{1,0:T(8,128)}), f32[48,2304]{1,0:T(8,128)}) %reduce-scatter.19.cloned.1.call-update) | async-done | bytes 442384
  712.7 174.4 %reduce-scatter.17.cloned.1.call-done = f32[192,768]{1,0:T(8,128)} async-done(((f32[3072,768]{1,0:T(8,128)}), f32[192,768]{1,0:T(8,128)}) %reduce-scatter.17.cloned.1.call-update) | async-done | bytes 589840 | tf_op jit(solution)/shard_map/reduce_scatter | solution.py:258
  888.9 173.7 %reduce-scatter.15.cloned.1.call-done = f32[48,3072]{1,0:T(8,128)} async-done(((f32[768,3072]{1,0:T(8,128)}), f32[48,3072]{1,0:T(8,128)}) %reduce-scatter.15.cloned.1.call-update) | async-done | bytes 589840 | tf_op jit(solution)/shard_map/reduce_scatter | solution.py:257
  1064.4 174.7 %reduce-scatter.13.cloned.1.call-done = f32[48,3072]{1,0:T(8,128)} async-done(((f32[768,3072]{1,0:T(8,128)}), f32[48,3072]{1,0:T(8,128)}) %reduce-scatter.13.cloned.1.call-update) | async-done | bytes 589840 | tf_op jit(solution)/shard_map/reduce_scatter | solution.py:256
  1242.3 122.2 %reduce-scatter.21.cloned.1.call-done = f32[48,4]{1,0:T(8,128)} async-done(((f32[768,4]{1,0:T(8,128)}), f32[48,4]{1,0:T(8,128)}) %reduce-scatter.21.cloned.1.call-update) | async-done | bytes 784
  1368.3 5.3 add_bitcast_fusion
  1373.6 14.7 %all-reduce.3.cloned.1.call-done = (bf16[48,2304]{0,1:T(8,128)(2,1)}, bf16[48,768]{1,0:T(8,128)(2,1)}, bf16[48,3072]{1,0:T(8,128)(2,1)}, bf16[48,3072]{1,0:T(8,128)(2,1)}, bf16[192,768]{1,0:T(8,128)(2,1)}) async-done(((bf16[48,2304]{0,1:T(8,128)(2,1)}, bf16[48,768]{1,0:T(8,128)(2,1)}, bf16[48,3072]{1,0:T(8,128)(2,1)}, bf16[48,3072]{1,0:T(8,128)(2,1)}, bf16[192,768]{1,0:T(8,128)(2,1)}), ...) | async-done | bytes 1179664 | tf_op jit(solution)/shard_map/psum | solution.py:262
  (422 shorter events, 362.1 us)
Async XLA Ops:
  7.2 586.3 %reduce-scatter.11.cloned.1.call-start = ((), (), s32[]{:S(2)}) async-start(), calls=%async_computation.6 | async-start | bytes 2506752 | tf_op jit(solution)/shard_map/reduce_scatter | solution.py:255
  15.5 21.6 %collective-permute-start.4 = (bf16[512,768]{1,0:T(8,128)(2,1)}, bf16[512,768]{1,0:T(8,128)(2,1)}, u32[]{:S(2)}, u32[]{:S(2)}) collective-permute-start(bf16[512,768]{1,0:T(8,128)(2,1)} %slice.177), channel_id=1, source_target_pairs={{0,1},{1,0},{2,3},{3,2},{4,5},{5,4},{6,7},{7,6},{8,9},{9,8},{10,11... | collective-permute-start | bytes 2359304 | tf_op jit(solution)/shard_map/ppermute | solution.py:15
  27.4 27.0 %copy-start.4 = (bf16[512,12,64]{0,2,1:T(8,128)(2,1)}, bf16[512,12,64]{0,2,1:T(8,128)(2,1)S(1)}, u32[]{:S(2)}) copy-start(bf16[512,12,64]{0,2,1:T(8,128)(2,1)S(1)} %maximum_convert_fusion) | copy-start | bytes 2359300
  27.4 28.8 %copy-start.44 = (s32[1,512]{1,0:T(1,128)S(1)}, s32[1,512]{1,0:T(1,128)}, u32[]{:S(2)}) copy-start(s32[1,512]{1,0:T(1,128)} %param.19) | copy-start | bytes 6148
  27.4 28.8 %copy-start.43 = (s32[1,512]{1,0:T(1,128)S(1)}, s32[1,512]{1,0:T(1,128)}, u32[]{:S(2)}) copy-start(s32[1,512]{1,0:T(1,128)} %param.18) | copy-start | bytes 6148
  27.4 25.6 %collective-permute-start.2 = (bf16[512,768]{0,1:T(8,128)(2,1)S(1)}, bf16[512,768]{0,1:T(8,128)(2,1)S(1)}, u32[]{:S(2)}, u32[]{:S(2)}) collective-permute-start(bf16[512,768]{0,1:T(8,128)(2,1)S(1)} %bitcast.217), channel_id=1, source_target_pairs={{0,1},{1,0},{2,3},{3,2},{4,5},{5,4},{6,7},{7,6},{8,9},{9,8},{10,11... | collective-permute-start | bytes 2359304 | tf_op jit(solution)/shard_map/ppermute | solution.py:15
  39.7 69.5 %collective-permute-start.5 = (bf16[1024,768]{1,0:T(8,128)(2,1)}, bf16[1024,768]{1,0:T(8,128)(2,1)}, u32[]{:S(2)}, u32[]{:S(2)}) collective-permute-start(bf16[1024,768]{1,0:T(8,128)(2,1)} %pad_maximum_fusion.3), channel_id=1, source_target_pairs={{0,2},{1,3},{2,0},{3,1},{4,6},{5,7},{6,4},{7,5},{8,10},{9,11},{10,... | collective-permute-start | bytes 4718600 | tf_op jit(solution)/shard_map/ppermute | solution.py:15
  54.4 69.8 %collective-permute-start.3 = (bf16[1024,768]{0,1:T(8,128)(2,1)}, bf16[1024,768]{0,1:T(8,128)(2,1)}, u32[]{:S(2)}, u32[]{:S(2)}) collective-permute-start(bf16[1024,768]{0,1:T(8,128)(2,1)} %pad_maximum_fusion.2), channel_id=1, source_target_pairs={{0,2},{1,3},{2,0},{3,1},{4,6},{5,7},{6,4},{7,5},{8,10},{9,11},{10,... | collective-permute-start | bytes 4718600 | tf_op jit(solution)/shard_map/ppermute | solution.py:15
  56.9 7.1 collective-permute-start
  64.0 44.6 %collective-permute-start.1 = (bf16[1024]{0:T(1024)(128)(2,1)S(1)}, bf16[1024]{0:T(1024)(128)(2,1)}, u32[]{:S(2)}, u32[]{:S(2)}) collective-permute-start(bf16[1024]{0:T(1024)(128)(2,1)S(1)} %pad_maximum_fusion.9), channel_id=1, source_target_pairs={{0,2},{1,3},{2,0},{3,1},{4,6},{5,7},{6,4},{7,5},{8,10},{9,11},{10,... | collective-permute-start | bytes 6152 | tf_op jit(solution)/shard_map/ppermute | solution.py:15
  223.1 44.1 %copy-start.32 = (f32[512]{0:T(512)}, f32[512]{0:T(512)S(1)}, u32[]{:S(2)}) copy-start(f32[512]{0:T(512)S(1)} %broadcast_multiply_fusion.4) | copy-start | bytes 6148
  223.4 43.8 %copy-start.36 = (f32[512]{0:T(512)}, f32[512]{0:T(512)S(1)}, u32[]{:S(2)}) copy-start(f32[512]{0:T(512)S(1)} %add_rsqrt_fusion.1) | copy-start | bytes 6148
  306.9 403.8 %reduce-scatter.19.cloned.1.call-start = ((), (), s32[]{:S(2)}) async-start(), calls=%async_computation.10 | async-start | bytes 7520256
  458.7 37.3 %collective-permute-start.6 = (bf16[1024,768]{0,1:T(8,128)(2,1)S(1)}, bf16[1024,768]{0,1:T(8,128)(2,1)S(1)}, u32[]{:S(2)}, u32[]{:S(2)}) collective-permute-start(bf16[1024,768]{0,1:T(8,128)(2,1)S(1)} %bitcast.235), channel_id=1, source_target_pairs={{0,2},{1,3},{2,0},{3,1},{4,6},{5,7},{6,4},{7,5},{8,10},{9,11},{10,... | collective-permute-start | bytes 4718600 | tf_op jit(solution)/shard_map/ppermute | solution.py:15
  461.3 67.6 %collective-permute-start.8 = (bf16[1024,768]{0,1:T(8,128)(2,1)S(1)}, bf16[1024,768]{0,1:T(8,128)(2,1)S(1)}, u32[]{:S(2)}, u32[]{:S(2)}) collective-permute-start(bf16[1024,768]{0,1:T(8,128)(2,1)S(1)} %bitcast.234), channel_id=1, source_target_pairs={{0,2},{1,3},{2,0},{3,1},{4,6},{5,7},{6,4},{7,5},{8,10},{9,11},{10,... | collective-permute-start | bytes 4718600 | tf_op jit(solution)/shard_map/ppermute | solution.py:15
  463.0 34.0 %slice-start.2 = ((s8[6291456]{0:T(1024)(128)(4,1)}), s8[4194304]{0:T(1024)(128)(4,1)S(1)}, s32[]{:S(2)}) async-start(s8[6291456]{0:T(1024)(128)(4,1)} %bitcast.225), calls=%async_computation.15 | async-start | bytes 8388608
  463.4 33.6 %slice-start.3 = ((s8[6291456]{0:T(1024)(128)(4,1)}), s8[2097152]{0:T(1024)(128)(4,1)S(1)}, s32[]{:S(2)}) async-start(s8[6291456]{0:T(1024)(128)(4,1)} %bitcast.225), calls=%async_computation.16 | async-start | bytes 4194304
  496.9 33.0 %collective-permute-start.7 = (bf16[512,768]{0,1:T(8,128)(2,1)S(1)}, bf16[512,768]{0,1:T(8,128)(2,1)S(1)}, u32[]{:S(2)}, u32[]{:S(2)}) collective-permute-start(bf16[512,768]{0,1:T(8,128)(2,1)S(1)} %slice.176), channel_id=1, source_target_pairs={{0,1},{1,0},{2,3},{3,2},{4,5},{5,4},{6,7},{7,6},{8,9},{9,8},{10,11... | collective-permute-start | bytes 2359304 | tf_op jit(solution)/shard_map/ppermute | solution.py:15
  529.9 18.8 %collective-permute-start.9 = (bf16[512,768]{0,1:T(8,128)(2,1)S(1)}, bf16[512,768]{0,1:T(8,128)(2,1)S(1)}, u32[]{:S(2)}, u32[]{:S(2)}) collective-permute-start(bf16[512,768]{0,1:T(8,128)(2,1)S(1)} %slice.175), channel_id=1, source_target_pairs={{0,1},{1,0},{2,3},{3,2},{4,5},{5,4},{6,7},{7,6},{8,9},{9,8},{10,11... | collective-permute-start | bytes 2359304 | tf_op jit(solution)/shard_map/ppermute | solution.py:15
  562.9 324.2 %reduce-scatter.17.cloned.1.call-start = ((), (), s32[]{:S(2)}) async-start(), calls=%async_computation.9 | async-start | bytes 10027008 | tf_op jit(solution)/shard_map/reduce_scatter | solution.py:258
  571.9 490.7 %reduce-scatter.15.cloned.1.call-start = ((), (), s32[]{:S(2)}) async-start(), calls=%async_computation.8 | async-start | bytes 10027008 | tf_op jit(solution)/shard_map/reduce_scatter | solution.py:257
  580.4 658.7 %reduce-scatter.13.cloned.1.call-start = ((), (), s32[]{:S(2)}) async-start(), calls=%async_computation.7 | async-start | bytes 10027008 | tf_op jit(solution)/shard_map/reduce_scatter | solution.py:256
  589.0 775.4 %reduce-scatter.21.cloned.1.call-start = ((), (), s32[]{:S(2)}) async-start(), calls=%async_computation.11 | async-start | bytes 417792
  593.4 794.9 %all-reduce.3.cloned.1.call-start = ((), (), s32[]{:S(2)}) async-start(), calls=%async_computation.12 | async-start | bytes 3096576 | tf_op jit(solution)/shard_map/psum | solution.py:262
  (65 other events, 323.5 us)
Sparse Core Ops, SparseCore 0:
  307.0 124.3 reduce-scatter.10
  563.0 147.6 reduce-scatter.18
  717.3 169.7 reduce-scatter.16
  892.6 169.8 reduce-scatter.14
  1069.1 170.0 reduce-scatter.12
  1244.2 120.2 reduce-scatter.20
  1368.5 19.7 all-reduce.2
where the time goes:
time: 1410 us
  waiting for transfers between devices  917 us (65%)
  matrix products  273 us (19%)
  local copies, waits for them, and re-layouts  83.7 us (6%)
  other arithmetic  55.8 us (4%)
  blocking collectives  46.3 us (3%)
  between operations  17.2 us (1%)
    unnamed x9, waiting for transfers between devices  238 us
    reduce_scatter x1, waiting for transfers between devices, local(): lax.psum_scatter(terms[2], 'dp', scatter_dimension=0, tiled=True)  175 us
    reduce_scatter x1, waiting for transfers between devices, local(): lax.psum_scatter(terms[4], 'dp', scatter_dimension=0, tiled=True)  174 us
    reduce_scatter x1, waiting for transfers between devices, local(): lax.psum_scatter(terms[3], 'dp', scatter_dimension=0, tiled=True)  174 us
    ppermute x10, waiting for transfers between devices, swapped(): lax.ppermute(value, axis, [(i, i ^ 1 << bit) for i in range(lax.axis_size...  142 us
    dot_general x41, matrix products, contract_last(): lax.dot_general(left, right, (((1,), (1,)), ((), ())), preferred_element_...  100 us
    dot_general x29, matrix products, contract_first(): lax.dot_general(left, right, (((0,), (0,)), ((), ())), preferred_element_...  85.5 us
    all_gather x1, blocking collectives, local(): part_sums = lax.all_gather(sums, 'dp', axis=0, tiled=True)  42 us
  transfers between devices with their start and end apart: 17, of which 12 were waited for; matrix products, arithmetic and copies ran while one was open for 18% of the time, Pallas kernels for 0%

commit v1 on v0

--- a/solution.py
+++ b/solution.py
@@ -157,7 +157,13 @@
     )
     sums = jnp.dot(member.T, second, precision=precise)
     group = place // SPAN
-    part_sums = lax.all_gather(sums, "dp", axis=0, tiled=True)
+    size = lax.axis_size("dp")
+    held, blocks = (sums, [sums])
+    for _ in range(size - 1):
+        held = lax.ppermute(held, "dp", [(i_2, (i_2 + 1) % size) for i_2 in range(size)])
+        blocks.insert(0, held)
+    row_of_blocks = jnp.concatenate(blocks, axis=0)
+    part_sums = jnp.roll(row_of_blocks, (lax.axis_index("dp") + 1) * sums.shape[0], axis=0)
     own_pooled = jnp.sum(part_sums.reshape(-1, SPAN, DOCS_GRP, width), 1).reshape(-1, width)
     own_embed = own_pooled * lax.rsqrt(jnp.sum(own_pooled * own_pooled, -1, keepdims=True) + 1e-06)
     embed = lax.all_gather(

time: 1410 us -> 1520 us (1.078)
  waiting for transfers between devices: 917 us -> 1030 us
  blocking collectives: 46.3 us -> 4.28 us
  local copies, waits for them, and re-layouts: 83.7 us -> 123 us
    ppermute x0 -> x15, waiting for transfers between devices: none -> 108 us  [local(): lax.ppermute(held, 'dp', [(i_2, (i_2 + 1) % size) for i_2 in range(size)])]
    all_gather x1 -> x0, blocking collectives: 42 us -> none  [local(): part_sums = lax.all_gather(sums, 'dp', axis=0, tiled=True)]
    concatenate x0 -> x1, local copies, waits for them, and re-layouts: none -> 27.8 us  [local(): jnp.roll(row_of_blocks, (lax.axis_index('dp') + 1) * sums.shape[0], axis=0)]
    unnamed x126 -> x152, local copies, waits for them, and re-layouts: 24.3 us -> 32 us
  transfers between devices with their start and end apart: 17 -> 32, of which waited for: 12 -> 27; matrix products, arithmetic and copies ran while one was open for 18% -> 17% of each run, Pallas kernels for 0% -> 0%
where the time goes in v1:
time: 1520 us; the launch traced here: 1510 us
  waiting for transfers between devices  1030 us (68%)
  matrix products  273 us (18%)
  local copies, waits for them, and re-layouts  123 us (8%)
  other arithmetic  58.2 us (4%)
  between operations  17.2 us (1%)
    unnamed x9, waiting for transfers between devices  238 us
    reduce_scatter x1, waiting for transfers between devices, local(): lax.psum_scatter(terms[2], 'dp', scatter_dimension=0, tiled=True)  174 us
    reduce_scatter x1, waiting for transfers between devices, local(): lax.psum_scatter(terms[4], 'dp', scatter_dimension=0, tiled=True)  174 us
    reduce_scatter x1, waiting for transfers between devices, local(): lax.psum_scatter(terms[3], 'dp', scatter_dimension=0, tiled=True)  174 us
    ppermute x10, waiting for transfers between devices, swapped(): lax.ppermute(value, axis, [(i, i ^ 1 << bit) for i in range(lax.axis_size...  142 us
    ppermute x15, waiting for transfers between devices, local(): lax.ppermute(held, 'dp', [(i_2, (i_2 + 1) % size) for i_2 in range(size)])  108 us
    dot_general x41, matrix products, contract_last(): lax.dot_general(left, right, (((1,), (1,)), ((), ())), preferred_element_...  100 us
    dot_general x29, matrix products, contract_first(): lax.dot_general(left, right, (((0,), (0,)), ((), ())), preferred_element_...  85.4 us
  transfers between devices with their start and end apart: 32, of which 27 were waited for; matrix products, arithmetic and copies ran while one was open for 17% of the time, Pallas kernels for 0%

profile of v1, /device:TPU:0, one launch (start us, length us, event | category | flops | bytes accessed | tf_op | source)
XLA Modules:
  0.0 1514.7 jit_solution(352229151834145395)
XLA Ops:
  27.5 9.6 collective-permute-done.4
  41.8 11.2 collective-permute-done.2
  68.3 40.3 %collective-permute-done.1 = bf16[1024]{0:T(1024)(128)(2,1)} collective-permute-done((bf16[1024]{0:T(1024)(128)(2,1)S(1)}, bf16[1024]{0:T(1024)(128)(2,1)}, u32[]{:S(2)}, u32[]{:S(2)}) %collective-permute-start.1) | collective-permute-done | bytes 2080 | tf_op jit(solution)/shard_map/ppermute | solution.py:15
  134.9 72.1 %while.28 = (s32[]{:T(128)}, bf16[12,1,512,64]{2,3,1,0:T(8,128)(2,1)}, f32[12,1,512]{2,1,0:T(1,128)}, f32[1,512]{1,0:T(1,128)S(1)}, f32[2048]{0:T(1024)S(1)}, /*...) while((s32[]{:T(128)}, ...), condition=%wide.region_3.4_spmd.clone, body=%wide.region_0.3_spmd.sunk.clone | while | flops 277872128 | bytes 13926497 | solution.py:142
  234.1 7.3 collective-permute-done.7
  242.0 7.3 collective-permute-done.8
  328.9 7.4 collective-permute-done.19
  336.4 7.5 collective-permute-done.20
  343.9 27.8 %concatenate.61 = f32[96,768]{1,0:T(8,128)} concatenate(f32[3,768]{1,0:T(4,128)} %collective-permute-done.20, f32[3,768]{1,0:T(4,128)} %collective-permute-done.19, f32[3,768]{1,0:T(4,128)} %copy-done.40, f32[3,768]{1,0:T(4,128)} %copy-done.39, f32[3,768]{1,0:T(4,128)} %copy-done.38, f32[3,768]{1,0:T(4,128)} %copy-done.37, f32[3,768]{1,0:T(4,128)} %copy-done.36, ...), dimensions={0} | concatenate | bytes 589824 | tf_op jit(solution)/shard_map/jit(_roll_dynamic)/concatenate | solution.py:166
  392.5 9.4 multiply_convert_fusion.1
  416.6 149.5 %while.29 = (s32[]{:T(128)}, f32[12,2048,64]{1,2,0:T(8,128)}, f32[12,2048,64]{1,2,0:T(8,128)}, f32[12,1,512,64]{2,3,1,0:T(8,128)}, f32[1,512]{1,0:T(1,128)}, /*i...) while((s32[]{:T(128)}, f32[12,2048,64]{1,2,0:T(8,128)}, ...), condition=%wide.region_22.23_spmd.clone, body=%wide.region_20.22_spmd.sunk.clone | while | flops 681737728 | bytes 34636948 | solution.py:236
  573.1 32.6 %collective-permute-done.21 = bf16[1024,768]{0,1:T(8,128)(2,1)S(1)} collective-permute-done((bf16[1024,768]{0,1:T(8,128)(2,1)S(1)}, bf16[1024,768]{0,1:T(8,128)(2,1)S(1)}, u32[]{:S(2)}, u32[]{:S(2)}) %collective-permute-start.21) | collective-permute-done | bytes 1572896 | tf_op jit(solution)/shard_map/ppermute | solution.py:15
  607.1 31.5 %collective-permute-done.23 = bf16[1024,768]{0,1:T(8,128)(2,1)S(1)} collective-permute-done((bf16[1024,768]{0,1:T(8,128)(2,1)S(1)}, bf16[1024,768]{0,1:T(8,128)(2,1)S(1)}, u32[]{:S(2)}, u32[]{:S(2)}) %collective-permute-start.23) | collective-permute-done | bytes 1572896 | tf_op jit(solution)/shard_map/ppermute | solution.py:15
  641.5 16.9 %collective-permute-done.24 = bf16[512,768]{0,1:T(8,128)(2,1)S(1)} collective-permute-done((bf16[512,768]{0,1:T(8,128)(2,1)S(1)}, bf16[512,768]{0,1:T(8,128)(2,1)S(1)}, u32[]{:S(2)}, u32[]{:S(2)}) %collective-permute-start.24) | collective-permute-done | bytes 786464 | tf_op jit(solution)/shard_map/ppermute | solution.py:15
  664.4 8.0 copy.64
  672.6 8.7 fusion.54
  681.4 8.4 fusion.98
  689.9 8.5 fusion.97
  704.5 115.7 %reduce-scatter.19.cloned.1.call-done = f32[48,2304]{1,0:T(8,128)} async-done(((f32[768,2304]{1,0:T(8,128)}), f32[48,2304]{1,0:T(8,128)}) %reduce-scatter.19.cloned.1.call-update) | async-done | bytes 442384
  822.3 174.4 %reduce-scatter.17.cloned.1.call-done = f32[192,768]{1,0:T(8,128)} async-done(((f32[3072,768]{1,0:T(8,128)}), f32[192,768]{1,0:T(8,128)}) %reduce-scatter.17.cloned.1.call-update) | async-done | bytes 589840 | tf_op jit(solution)/shard_map/reduce_scatter | solution.py:264
  998.5 173.6 %reduce-scatter.15.cloned.1.call-done = f32[48,3072]{1,0:T(8,128)} async-done(((f32[768,3072]{1,0:T(8,128)}), f32[48,3072]{1,0:T(8,128)}) %reduce-scatter.15.cloned.1.call-update) | async-done | bytes 589840 | tf_op jit(solution)/shard_map/reduce_scatter | solution.py:263
  1173.9 174.4 %reduce-scatter.13.cloned.1.call-done = f32[48,3072]{1,0:T(8,128)} async-done(((f32[768,3072]{1,0:T(8,128)}), f32[48,3072]{1,0:T(8,128)}) %reduce-scatter.13.cloned.1.call-update) | async-done | bytes 589840 | tf_op jit(solution)/shard_map/reduce_scatter | solution.py:262
  1351.5 122.2 %reduce-scatter.21.cloned.1.call-done = f32[48,4]{1,0:T(8,128)} async-done(((f32[768,4]{1,0:T(8,128)}), f32[48,4]{1,0:T(8,128)}) %reduce-scatter.21.cloned.1.call-update) | async-done | bytes 784
  1482.8 14.7 all-reduce.3.cloned.1.call-done
  (480 shorter events, 479.8 us)
Async XLA Ops:
  7.2 695.7 %reduce-scatter.11.cloned.1.call-start = ((), (), s32[]{:S(2)}) async-start(), calls=%async_computation.6 | async-start | bytes 2506752 | tf_op jit(solution)/shard_map/reduce_scatter | solution.py:261
  15.5 21.6 %collective-permute-start.4 = (bf16[512,768]{1,0:T(8,128)(2,1)}, bf16[512,768]{1,0:T(8,128)(2,1)}, u32[]{:S(2)}, u32[]{:S(2)}) collective-permute-start(bf16[512,768]{1,0:T(8,128)(2,1)} %slice.177), channel_id=1, source_target_pairs={{0,1},{1,0},{2,3},{3,2},{4,5},{5,4},{6,7},{7,6},{8,9},{9,8},{10,11... | collective-permute-start | bytes 2359304 | tf_op jit(solution)/shard_map/ppermute | solution.py:15
  27.4 25.6 %collective-permute-start.2 = (bf16[512,768]{0,1:T(8,128)(2,1)S(1)}, bf16[512,768]{0,1:T(8,128)(2,1)S(1)}, u32[]{:S(2)}, u32[]{:S(2)}) collective-permute-start(bf16[512,768]{0,1:T(8,128)(2,1)S(1)} %bitcast.213), channel_id=1, source_target_pairs={{0,1},{1,0},{2,3},{3,2},{4,5},{5,4},{6,7},{7,6},{8,9},{9,8},{10,11... | collective-permute-start | bytes 2359304 | tf_op jit(solution)/shard_map/ppermute | solution.py:15
  39.8 69.5 %collective-permute-start.5 = (bf16[1024,768]{1,0:T(8,128)(2,1)}, bf16[1024,768]{1,0:T(8,128)(2,1)}, u32[]{:S(2)}, u32[]{:S(2)}) collective-permute-start(bf16[1024,768]{1,0:T(8,128)(2,1)} %pad_maximum_fusion.3), channel_id=1, source_target_pairs={{0,2},{1,3},{2,0},{3,1},{4,6},{5,7},{6,4},{7,5},{8,10},{9,11},{10,... | collective-permute-start | bytes 4718600 | tf_op jit(solution)/shard_map/ppermute | solution.py:15
  54.6 69.7 %collective-permute-start.3 = (bf16[1024,768]{0,1:T(8,128)(2,1)}, bf16[1024,768]{0,1:T(8,128)(2,1)}, u32[]{:S(2)}, u32[]{:S(2)}) collective-permute-start(bf16[1024,768]{0,1:T(8,128)(2,1)} %pad_maximum_fusion.2), channel_id=1, source_target_pairs={{0,2},{1,3},{2,0},{3,1},{4,6},{5,7},{6,4},{7,5},{8,10},{9,11},{10,... | collective-permute-start | bytes 4718600 | tf_op jit(solution)/shard_map/ppermute | solution.py:15
  64.1 44.4 %collective-permute-start.1 = (bf16[1024]{0:T(1024)(128)(2,1)S(1)}, bf16[1024]{0:T(1024)(128)(2,1)}, u32[]{:S(2)}, u32[]{:S(2)}) collective-permute-start(bf16[1024]{0:T(1024)(128)(2,1)S(1)} %pad_maximum_fusion.9), channel_id=1, source_target_pairs={{0,2},{1,3},{2,0},{3,1},{4,6},{5,7},{6,4},{7,5},{8,10},{9,11},{10,... | collective-permute-start | bytes 6152 | tf_op jit(solution)/shard_map/ppermute | solution.py:15
  226.2 7.3 collective-permute-start.6
  234.1 7.3 collective-permute-start.7
  242.0 7.3 collective-permute-start.8
  249.8 7.3 collective-permute-start.9
  257.7 7.3 collective-permute-start.10
  305.1 7.5 collective-permute-start.16
  328.9 7.4 collective-permute-start.19
  336.3 7.6 collective-permute-start.20
  416.1 404.1 %reduce-scatter.19.cloned.1.call-start = ((), (), s32[]{:S(2)}) async-start(), calls=%async_computation.10 | async-start | bytes 7520256
  568.4 37.3 %collective-permute-start.21 = (bf16[1024,768]{0,1:T(8,128)(2,1)S(1)}, bf16[1024,768]{0,1:T(8,128)(2,1)S(1)}, u32[]{:S(2)}, u32[]{:S(2)}) collective-permute-start(bf16[1024,768]{0,1:T(8,128)(2,1)S(1)} %bitcast.231), channel_id=1, source_target_pairs={{0,2},{1,3},{2,0},{3,1},{4,6},{5,7},{6,4},{7,5},{8,10},{9,11},{10,... | collective-permute-start | bytes 4718600 | tf_op jit(solution)/shard_map/ppermute | solution.py:15
  571.0 67.6 %collective-permute-start.23 = (bf16[1024,768]{0,1:T(8,128)(2,1)S(1)}, bf16[1024,768]{0,1:T(8,128)(2,1)S(1)}, u32[]{:S(2)}, u32[]{:S(2)}) collective-permute-start(bf16[1024,768]{0,1:T(8,128)(2,1)S(1)} %bitcast.230), channel_id=1, source_target_pairs={{0,2},{1,3},{2,0},{3,1},{4,6},{5,7},{6,4},{7,5},{8,10},{9,11},{10,... | collective-permute-start | bytes 4718600 | tf_op jit(solution)/shard_map/ppermute | solution.py:15
  606.6 33.0 %collective-permute-start.22 = (bf16[512,768]{0,1:T(8,128)(2,1)S(1)}, bf16[512,768]{0,1:T(8,128)(2,1)S(1)}, u32[]{:S(2)}, u32[]{:S(2)}) collective-permute-start(bf16[512,768]{0,1:T(8,128)(2,1)S(1)} %slice.176), channel_id=1, source_target_pairs={{0,1},{1,0},{2,3},{3,2},{4,5},{5,4},{6,7},{7,6},{8,9},{9,8},{10,11... | collective-permute-start | bytes 2359304 | tf_op jit(solution)/shard_map/ppermute | solution.py:15
  639.5 18.8 %collective-permute-start.24 = (bf16[512,768]{0,1:T(8,128)(2,1)S(1)}, bf16[512,768]{0,1:T(8,128)(2,1)S(1)}, u32[]{:S(2)}, u32[]{:S(2)}) collective-permute-start(bf16[512,768]{0,1:T(8,128)(2,1)S(1)} %slice.175), channel_id=1, source_target_pairs={{0,1},{1,0},{2,3},{3,2},{4,5},{5,4},{6,7},{7,6},{8,9},{9,8},{10,11... | collective-permute-start | bytes 2359304 | tf_op jit(solution)/shard_map/ppermute | solution.py:15
  672.4 324.3 %reduce-scatter.17.cloned.1.call-start = ((), (), s32[]{:S(2)}) async-start(), calls=%async_computation.9 | async-start | bytes 10027008 | tf_op jit(solution)/shard_map/reduce_scatter | solution.py:264
  681.3 490.8 %reduce-scatter.15.cloned.1.call-start = ((), (), s32[]{:S(2)}) async-start(), calls=%async_computation.8 | async-start | bytes 10027008 | tf_op jit(solution)/shard_map/reduce_scatter | solution.py:263
  689.9 658.5 %reduce-scatter.13.cloned.1.call-start = ((), (), s32[]{:S(2)}) async-start(), calls=%async_computation.7 | async-start | bytes 10027008 | tf_op jit(solution)/shard_map/reduce_scatter | solution.py:262
  698.5 775.2 %reduce-scatter.21.cloned.1.call-start = ((), (), s32[]{:S(2)}) async-start(), calls=%async_computation.11 | async-start | bytes 417792
  702.8 794.7 %all-reduce.3.cloned.1.call-start = ((), (), s32[]{:S(2)}) async-start(), calls=%async_computation.12 | async-start | bytes 3096576 | tf_op jit(solution)/shard_map/psum | solution.py:268
  (93 other events, 766.8 us)
Sparse Core Ops, SparseCore 0:
  416.3 124.3 reduce-scatter.10
  672.5 147.6 reduce-scatter.18
  826.8 169.7 reduce-scatter.16
  1002.2 169.8 reduce-scatter.14
  1178.6 169.7 reduce-scatter.12
  1353.4 120.2 reduce-scatter.20
  1477.8 19.7 all-reduce.2
